TPU v7x, 32 devices: a whole 2x2x4 slice. The times are simulated.
32 devices in a mesh: row: 4 (over y, core), col: 8 (over z, x).
Axes of the slice: x: 2, y: 2, z: 4, core: 2. Of those that a mesh axis runs over, the one named last changes fastest.
Arguments:
- rhs_tile: float32 [18432, 9216], P('row', 'col'), may hold values from -6 to 6
- factor: float32 [18432, 1536], P('row', 'col'), may hold values from -1 to 2.5, as said below
Outputs:
- whitened: float32 [18432, 9216], P('row', 'col')
Inputs may be any that keep to these rules, and one draw needn't show every extreme that they name: In elimination order factor is lower triangular: entries above the diagonal are zero, diagonal entries are at least 0.7.
All inputs are finite; a program needn't handle non-finite values.
Results may differ from a plain program's by a relative error of at most 0.0001.
Values sent between devices are 32-bit elements; how exact they have to be, the bound alone decides.
A program may use at most 128 MiB of HBM per device.

v0:
```python
import jax
import jax.numpy as jnp
from jax import lax
from jax.sharding import PartitionSpec as P

PANEL = 512
PANELS = 3


def local(rhs_tile, factor):
    row_count = lax.axis_size("row")
    col_count = lax.axis_size("col")
    row_piece = PANEL // row_count
    col_piece = PANEL // col_count
    my_row = lax.axis_index("row")
    result = rhs_tile
    for panel_index in range(PANELS):
        start_row = panel_index * row_piece
        end_row = start_row + row_piece
        first_col = panel_index * col_piece
        strip = lax.all_gather(
            factor[start_row:end_row, first_col : first_col + col_piece], "col", axis=1, tiled=True
        )
        diagonal = lax.all_gather(strip, "row", axis=0, tiled=True)
        own_rows = result[start_row:end_row]
        stacked = lax.all_gather(own_rows, "row", axis=0, tiled=True)
        solved = jax.scipy.linalg.solve_triangular(diagonal, stacked, lower=True)
        mine_rows = lax.dynamic_slice_in_dim(solved, my_row * row_piece, row_piece, 0)
        trailing = result[end_row:]

        def add_panel(total, piece, start, solved=solved):
            return jnp.dot(
                piece, solved, precision=lax.Precision.HIGHEST, preferred_element_type=jnp.float32
            )

        initial = jnp.zeros(trailing.shape, jnp.float32)
        update = add_panel(
            initial,
            lax.all_gather(
                factor[end_row:, first_col : first_col + col_piece], "col", axis=1, tiled=True
            ),
            jnp.int32(0),
        )
        result = jnp.concatenate([result[:start_row], mine_rows, trailing - update], axis=0)
    return result


def solution(mesh):
    in_specs = (P("row", "col"), P("row", "col"))
    out_specs = P("row", "col")
    return jax.shard_map(local, mesh=mesh, in_specs=in_specs, out_specs=out_specs, check_vma=False)
```

profile of v0, /device:TPU:0, one launch (start us, length us, event | category | flops | bytes accessed | tf_op | source)
XLA Modules:
  0.0 708.7 jit_solution(17606545993645377573)
XLA Ops:
  7.3 34.5 %all_gather.36 = f32[128,512]{0,1:T(8,128)} all-gather(f32[128,64]{0,1:T(8,128)S(1)} %get-tuple-element.73), channel_id=1, replica_groups=mesh['row'=4,'col'=8] {'col'}, dimensions={1}, use_global_device_ids=true | all-gather | bytes 294912 | tf_op jit(solution)/shard_map/all_gather | solution.py:21
  42.0 1.9 slice.59
  44.0 2.4 slice.62
  46.4 32.8 %all_gather.39 = f32[128,512]{0,1:T(8,128)} all-gather(f32[128,64]{0,1:T(8,128)S(1)} %get-tuple-element.72), channel_id=1, replica_groups=mesh['row'=4,'col'=8] {'col'}, dimensions={1}, use_global_device_ids=true | all-gather | bytes 294912 | tf_op jit(solution)/shard_map/all_gather | solution.py:21
  79.2 15.6 %slice.61 = f32[4480,1152]{1,0:T(8,128)} slice(f32[4608,1152]{1,0:T(8,128)} %param.4), slice={[128:4608], [0:1152]} | slice | bytes 41287680 | tf_op jit(solution)/shard_map/slice | solution.py:29
  94.8 22.6 %copy.36 = f32[4480,1152]{0,1:T(8,128)} copy(f32[4480,1152]{1,0:T(8,128)} %slice.61) | data formatting | bytes 41287680
  118.9 8.5 %while.6 = (s32[]{:T(128)}, f32[512,512]{0,1:T(8,128)S(1)}, s32[4,2]{0,1:T(2,128)S(1)}, f32[4,128,128]{2,1,0:T(8,128)S(1)}, s32[]{:T(128)}) while((s32[]{:T(128)}, f32[512,512]{0,1:T(8,128)S(1)}, s32[4,2]{0,1:T(2,128)S(1)}, f32[4,128,128]{2,1,0:T(8,128)S(1)}, s32[]{:T(128)}) %tuple.54), condition=%wide.while_cond, body=%wide.while_body.sunk | while | flops 2 | bytes 393321 | solution.py:27
  127.4 39.3 %custom-call.5 = f32[4,128,128]{1,2,0:T(8,128)S(1)} custom-call(f32[4,128,128]{2,1,0:T(8,128)S(1)} %get-tuple-element.26), custom_call_target="InvertDiagBlocksLowerTriangular" | custom-call | tf_op jit(solution)/shard_map/jit(_solve_triangular)/triangular_solve | solution.py:27
  166.8 1.9 fusion.34
  168.7 1.7 convolution_subtract_fusion.8
  172.6 2.2 convolution_subtract_fusion.2
  175.6 46.5 %all-gather.16.cloned.1.call-done = f32[4480,512]{0,1:T(8,128)} async-done(((f32[4480,64]{0,1:T(8,128)}), f32[4480,512]{0,1:T(8,128)}) %all-gather.16.cloned.1.call-update) | async-done | bytes 9175056 | tf_op jit(solution)/shard_map/all_gather | solution.py:39
  222.1 41.0 %fusion = f32[4480,1152]{0,1:T(8,128)S(1)} fusion(f32[4480,1152]{0,1:T(8,128)} %copy.36, f32[4480,512]{0,1:T(8,128)} %all-gather.16.cloned.1.call-done, f32[128,1152]{1,0:T(8,128)S(1)} %fusion.50, f32[128,1152]{1,0:T(8,128)S(1)} %fusion.51, f32[128,1152]{1,0:T(8,128)S(1)} %fusion.53, f32[128,1152]{1,0:T(8,128)S(1)} %fusion.34), kind=kOutput, calls=%fused_computation.9 | convolution fusion | flops 31715868672 | bytes 52822016 | tf_op jit(solution)/shard_map/dot_general | solution.py:32
  263.1 7.4 %copy-done = f32[4480,1152]{0,1:T(8,128)} copy-done((f32[4480,1152]{0,1:T(8,128)}, f32[4480,1152]{0,1:T(8,128)S(1)}, u32[]{:S(2)}) %copy-start) | copy-done | bytes 20643864
  271.5 2.3 slice.66
  274.0 32.8 %all_gather.43 = f32[128,512]{0,1:T(8,128)} all-gather(f32[128,64]{0,1:T(8,128)S(1)} %get-tuple-element.71), channel_id=1, replica_groups=mesh['row'=4,'col'=8] {'col'}, dimensions={1}, use_global_device_ids=true | all-gather | bytes 294912 | tf_op jit(solution)/shard_map/all_gather | solution.py:21
  306.8 2.3 fusion.28
  309.2 12.3 %while.7 = (s32[]{:T(128)}, f32[512,512]{0,1:T(8,128)}, s32[4,2]{0,1:T(2,128)S(1)}, f32[4,128,128]{2,1,0:T(8,128)S(1)}, s32[]{:T(128)}) while((s32[]{:T(128)}, f32[512,512]{0,1:T(8,128)}, s32[4,2]{0,1:T(2,128)S(1)}, f32[4,128,128]{2,1,0:T(8,128)S(1)}, s32[]{:T(128)}) %tuple.81), condition=%wide.while_cond.clone, body=%wide.while_body.clone.sunk | while | flops 2 | bytes 393321 | solution.py:27
  310.3 2.2 dynamic-slice.19
  313.3 2.2 dynamic-slice.19
  316.2 2.2 dynamic-slice.19
  319.2 2.1 dynamic-slice.19
  321.5 39.3 %custom-call.6 = f32[4,128,128]{1,2,0:T(8,128)S(1)} custom-call(f32[4,128,128]{2,1,0:T(8,128)S(1)} %get-tuple-element.27), custom_call_target="InvertDiagBlocksLowerTriangular" | custom-call | tf_op jit(solution)/shard_map/jit(_solve_triangular)/triangular_solve | solution.py:27
  360.9 1.9 fusion.32
  363.8 2.2 convolution_subtract_fusion.6
  367.8 3.2 convolution_subtract_fusion.5
  371.0 1.6 fusion.47
  373.6 4.3 convolution_subtract_fusion.1
  379.3 47.6 %all-gather.22.cloned.1.call-done = f32[4352,512]{0,1:T(8,128)} async-done(((f32[4352,64]{0,1:T(8,128)}), f32[4352,512]{0,1:T(8,128)}) %all-gather.22.cloned.1.call-update) | async-done | bytes 8912912 | tf_op jit(solution)/shard_map/all_gather | solution.py:39
  426.9 41.9 %fusion.2 = f32[4352,1152]{0,1:T(8,128)} fusion(f32[4352,512]{0,1:T(8,128)} %all-gather.22.cloned.1.call-done, f32[4480,1152]{0,1:T(8,128)} %copy-done, f32[128,1152]{0,1:T(8,128)S(1)} %fusion.46, f32[128,1152]{0,1:T(8,128)} %copy.22, f32[128,1152]{0,1:T(8,128)} %copy.21, f32[128,1152]{0,1:T(8,128)} %copy.20), kind=kOutput, calls=%fused_computation.11 | convolution fusion | flops 30809751552 | bytes 51380224 | tf_op jit(solution)/shard_map/dot_general | solution.py:32
  468.8 1.9 slice.87
  470.8 2.3 slice.69
  473.1 2.4 fusion.27
  475.5 12.0 %while.8 = (s32[]{:T(128)}, f32[512,512]{0,1:T(8,128)}, s32[4,2]{0,1:T(2,128)S(1)}, f32[4,128,128]{2,1,0:T(8,128)S(1)}, s32[]{:T(128)}) while((s32[]{:T(128)}, f32[512,512]{0,1:T(8,128)}, s32[4,2]{0,1:T(2,128)S(1)}, f32[4,128,128]{2,1,0:T(8,128)S(1)}, s32[]{:T(128)}) %tuple.82), condition=%wide.while_cond.clone.1, body=%wide.while_body.clone.1.sunk | while | flops 2 | bytes 393321 | solution.py:27
  476.2 2.2 dynamic-slice.21
  479.2 2.2 dynamic-slice.21
  482.3 2.2 dynamic-slice.21
  485.3 2.2 dynamic-slice.21
  487.5 40.1 %custom-call.7 = f32[4,128,128]{1,2,0:T(8,128)} custom-call(f32[4,128,128]{2,1,0:T(8,128)S(1)} %get-tuple-element.28), custom_call_target="InvertDiagBlocksLowerTriangular" | custom-call | tf_op jit(solution)/shard_map/jit(_solve_triangular)/triangular_solve | solution.py:27
  530.6 1.8 fusion.30
  532.6 2.2 convolution_subtract_fusion.4
  535.8 3.2 convolution_subtract_fusion.3
  538.9 1.6 fusion.43
  540.7 4.3 convolution_subtract_fusion
  547.6 75.9 %all-gather.26.cloned.1.call-done = f32[4224,512]{0,1:T(8,128)} async-done(((f32[4224,64]{0,1:T(8,128)}), f32[4224,512]{0,1:T(8,128)}) %all-gather.26.cloned.1.call-update) | async-done | bytes 8650768 | tf_op jit(solution)/shard_map/all_gather | solution.py:39
  623.5 41.2 %fusion.1 = f32[4224,1152]{0,1:T(8,128)} fusion(f32[4224,512]{0,1:T(8,128)} %all-gather.26.cloned.1.call-done, f32[4352,1152]{0,1:T(8,128)} %fusion.2, f32[128,1152]{0,1:T(8,128)S(1)} %fusion.42, f32[128,1152]{0,1:T(8,128)S(1)} %copy.27, f32[128,1152]{0,1:T(8,128)S(1)} %copy.26, f32[128,1152]{0,1:T(8,128)S(1)} %copy.25), kind=kOutput, calls=%fused_computation.10 | convolution fusion | flops 29903634432 | bytes 49938432 | tf_op jit(solution)/shard_map/dot_general | solution.py:32
  664.7 15.0 %pad_maximum_fusion = f32[4608,1152]{0,1:T(8,128)} fusion(f32[4224,1152]{0,1:T(8,128)} %fusion.1, f32[128,1152]{0,1:T(8,128)S(1)} %copy-done.10, f32[128,1152]{0,1:T(8,128)S(1)} %copy-done.9, f32[128,1152]{0,1:T(8,128)S(1)} %copy-done.8), kind=kLoop, calls=%fused_computation.12 | loop fusion | flops 15925248 | bytes 42467328 | tf_op jit(solution)/shard_map/concatenate | solution.py:44
  679.7 22.1 %copy.30 = f32[4608,1152]{1,0:T(8,128)} copy(f32[4608,1152]{0,1:T(8,128)} %pad_maximum_fusion) | data formatting | bytes 42467328 | tf_op jit(solution)/shard_map/concatenate | solution.py:44
  (130 shorter events, 33.2 us)
Async XLA Ops:
  6.5 110.9 %all-gather.10.cloned.1.call-start = ((), (), s32[]{:S(2)}) async-start(), calls=%async_computation | async-start | bytes 1310720 | tf_op jit(solution)/shard_map/all_gather | solution.py:24
  41.9 124.9 %all-gather.12.cloned.1.call-start = ((), (), s32[]{:S(2)}) async-start(), calls=%async_computation.1 | async-start | bytes 2949120 | tf_op jit(solution)/shard_map/all_gather | solution.py:26
  43.9 178.2 %all-gather.16.cloned.1.call-start = ((), (), s32[]{:S(2)}) async-start(), calls=%async_computation.3 | async-start | bytes 10321920 | tf_op jit(solution)/shard_map/all_gather | solution.py:39
  46.3 260.5 %all-gather.14.cloned.1.call-start = ((), (), s32[]{:S(2)}) async-start(), calls=%async_computation.2 | async-start | bytes 1310720 | tf_op jit(solution)/shard_map/all_gather | solution.py:24
  79.2 281.7 %all-gather.18.cloned.1.call-start = ((), (), s32[]{:S(2)}) async-start(), calls=%async_computation.4 | async-start | bytes 2949120 | tf_op jit(solution)/shard_map/all_gather | solution.py:26
  127.4 43.7 %copy-start.6 = (f32[512,512]{0,1:T(8,128)}, f32[512,512]{0,1:T(8,128)S(1)}, u32[]{:S(2)}) copy-start(f32[512,512]{0,1:T(8,128)S(1)} %get-tuple-element.226) | copy-start | bytes 3145732
  166.8 4.3 copy-start.7
  175.6 87.6 %copy-start.1 = (f32[128,1152]{1,0:T(8,128)}, f32[128,1152]{1,0:T(8,128)S(1)}, u32[]{:S(2)}) copy-start(f32[128,1152]{1,0:T(8,128)S(1)} %fusion.50) | copy-start | bytes 1769476
  263.1 7.4 %copy-start = (f32[4480,1152]{0,1:T(8,128)}, f32[4480,1152]{0,1:T(8,128)S(1)}, u32[]{:S(2)}) copy-start(f32[4480,1152]{0,1:T(8,128)S(1)} %fusion) | copy-start | bytes 61931524
  271.5 155.4 %all-gather.22.cloned.1.call-start = ((), (), s32[]{:S(2)}) async-start(), calls=%async_computation.6 | async-start | bytes 10027008 | tf_op jit(solution)/shard_map/all_gather | solution.py:39
  273.9 199.2 %all-gather.20.cloned.1.call-start = ((), (), s32[]{:S(2)}) async-start(), calls=%async_computation.5 | async-start | bytes 1310720 | tf_op jit(solution)/shard_map/all_gather | solution.py:24
  306.8 223.8 %all-gather.24.cloned.1.call-start = ((), (), s32[]{:S(2)}) async-start(), calls=%async_computation.7 | async-start | bytes 2949120 | tf_op jit(solution)/shard_map/all_gather | solution.py:26
  360.8 5.9 copy-start.12
  470.7 152.7 %all-gather.26.cloned.1.call-start = ((), (), s32[]{:S(2)}) async-start(), calls=%async_computation.8 | async-start | bytes 9732096 | tf_op jit(solution)/shard_map/all_gather | solution.py:39
  473.1 54.6 %copy-start.2 = (f32[128,1152]{1,0:T(8,128)S(1)}, f32[128,1152]{1,0:T(8,128)}, u32[]{:S(2)}) copy-start(f32[128,1152]{1,0:T(8,128)} %copy-done.1) | copy-start | bytes 1769476
  527.9 1.2 copy-start.3
  527.9 1.3 copy-start.4
  527.9 1.6 copy-start.5
  529.5 1.1 copy-start.11
  547.6 117.1 %copy-start.8 = (f32[128,1152]{0,1:T(8,128)S(1)}, f32[128,1152]{0,1:T(8,128)}, u32[]{:S(2)}) copy-start(f32[128,1152]{0,1:T(8,128)} %copy.29) | copy-start | bytes 1769476
  547.6 117.1 %copy-start.9 = (f32[128,1152]{0,1:T(8,128)S(1)}, f32[128,1152]{0,1:T(8,128)}, u32[]{:S(2)}) copy-start(f32[128,1152]{0,1:T(8,128)} %constant_dynamic-slice_fusion.4) | copy-start | bytes 1769476
  623.5 41.2 %copy-start.10 = (f32[128,1152]{0,1:T(8,128)S(1)}, f32[128,1152]{0,1:T(8,128)}, u32[]{:S(2)}) copy-start(f32[128,1152]{0,1:T(8,128)} %constant_dynamic-slice_fusion.3) | copy-start | bytes 1769476
Sparse Core Ops, SparseCore 0:
  42.0 17.7 all-gather.9
  61.3 24.0 all-gather.11
  87.6 134.4 all-gather.15
  223.5 14.9 all-gather.13
  271.6 22.4 all-gather.17
  296.1 130.7 all-gather.21
  428.5 15.0 all-gather.19
  470.8 22.7 all-gather.23
  495.8 127.5 all-gather.25
where the time goes:
time: 718 us; the launch traced here: 709 us
  waiting for transfers between devices  170 us (24%)
  matrix products  163 us (23%)
  other arithmetic  140 us (19%)
  local copies, waits for them, and re-layouts  120 us (17%)
  blocking collectives  100 us (14%)
  between operations  14.1 us (2%)
    all_gather x3, waiting for transfers between devices, local(): lax.all_gather(factor[end_row:, first_col:first_col + col_piece], 'col',...  170 us
    another operation x10, other arithmetic, local(): solved = jax.scipy.linalg.solve_triangular(diagonal, stacked, lower=True)  125 us
    dot_general x3, matrix products, add_panel(): jnp.dot(piece, solved, precision=lax.Precision.HIGHEST, preferred_element...  124 us
    all_gather x3, blocking collectives, local(): lax.all_gather(factor[start_row:end_row, first_col:first_col + col_piece]...  100 us
    another operation x21, matrix products, local(): solved = jax.scipy.linalg.solve_triangular(diagonal, stacked, lower=True)  39.1 us
    another operation x70, local copies, waits for them, and re-layouts, local(): solved = jax.scipy.linalg.solve_triangular(diagonal, stacked, lower=True)  36 us
    unnamed x27, local copies, waits for them, and re-layouts  30.6 us
    concatenate x1, local copies, waits for them, and re-layouts, local(): jnp.concatenate([result[:start_row], mine_rows, trailing - update], axis=0)  22.1 us
  transfers between devices with their start and end apart: 9, of which 3 were waited for; matrix products, arithmetic and copies ran while one was open for 47% of the time, Pallas kernels for 0%

commit v1 on v0

--- a/solution.py
+++ b/solution.py
@@ -36,8 +36,8 @@
         initial = jnp.zeros(trailing.shape, jnp.float32)
         update = add_panel(
             initial,
-            lax.all_gather(
-                factor[end_row:, first_col : first_col + col_piece], "col", axis=1, tiled=True
+            jnp.concatenate(
+                lax.all_gather(factor[end_row:, first_col : first_col + col_piece], "col"), axis=1
             ),
             jnp.int32(0),
         )

time: 718 us -> 683 us (0.951)
  waiting for transfers between devices: 170 us -> 102 us
  local copies, waits for them, and re-layouts: 120 us -> 151 us
    all_gather x3, waiting for transfers between devices: 170 us -> 76.9 us  [local(): lax.all_gather(factor[end_row:, first_col:first_col + col_piece], 'col')]
    all_gather x3, waiting for transfers between devices: 0.04 us -> 24.8 us  [local(): stacked = lax.all_gather(own_rows, 'row', axis=0, tiled=True)]
    reshape x0 -> x3, local copies, waits for them, and re-layouts: none -> 16.5 us  [local(): jnp.concatenate(lax.all_gather(factor[end_row:, first_col:first_col + col...]
    unnamed x27 -> x36, local copies, waits for them, and re-layouts: 30.6 us -> 46.5 us
  transfers between devices with their start and end apart: 9 -> 9, of which waited for: 3 -> 5; matrix products, arithmetic and copies ran while one was open for 47% -> 52% of each run, Pallas kernels for 0% -> 0%
where the time goes in v1:
time: 683 us; the launch traced here: 671 us
  matrix products  163 us (24%)
  local copies, waits for them, and re-layouts  151 us (22%)
  other arithmetic  140 us (20%)
  blocking collectives  102 us (15%)
  waiting for transfers between devices  102 us (15%)
  between operations  13.9 us (2%)
    another operation x10, other arithmetic, local(): solved = jax.scipy.linalg.solve_triangular(diagonal, stacked, lower=True)  125 us
    dot_general x3, matrix products, add_panel(): jnp.dot(piece, solved, precision=lax.Precision.HIGHEST, preferred_element...  124 us
    all_gather x3, blocking collectives, local(): lax.all_gather(factor[start_row:end_row, first_col:first_col + col_piece]...  102 us
    all_gather x3, waiting for transfers between devices, local(): lax.all_gather(factor[end_row:, first_col:first_col + col_piece], 'col')  76.9 us
    unnamed x36, local copies, waits for them, and re-layouts  46.5 us
    another operation x21, matrix products, local(): solved = jax.scipy.linalg.solve_triangular(diagonal, stacked, lower=True)  39 us
    another operation x70, local copies, waits for them, and re-layouts, local(): solved = jax.scipy.linalg.solve_triangular(diagonal, stacked, lower=True)  35.4 us
    all_gather x3, waiting for transfers between devices, local(): stacked = lax.all_gather(own_rows, 'row', axis=0, tiled=True)  24.8 us
  transfers between devices with their start and end apart: 9, of which 5 were waited for; matrix products, arithmetic and copies ran while one was open for 52% of the time, Pallas kernels for 0%

profile of v1, /device:TPU:0, one launch (start us, length us, event | category | flops | bytes accessed | tf_op | source)
XLA Modules:
  0.0 671.3 jit_solution(6092020204747885236)
XLA Ops:
  7.3 34.5 %all_gather.45 = f32[128,512]{0,1:T(8,128)} all-gather(f32[128,64]{0,1:T(8,128)S(1)} %get-tuple-element.73), channel_id=1, replica_groups=mesh['row'=4,'col'=8] {'col'}, dimensions={1}, use_global_device_ids=true | all-gather | bytes 294912 | tf_op jit(solution)/shard_map/all_gather | solution.py:21
  44.0 2.3 slice.62
  46.4 32.8 %all_gather.48 = f32[128,512]{0,1:T(8,128)} all-gather(f32[128,64]{0,1:T(8,128)S(1)} %get-tuple-element.72), channel_id=1, replica_groups=mesh['row'=4,'col'=8] {'col'}, dimensions={1}, use_global_device_ids=true | all-gather | bytes 294912 | tf_op jit(solution)/shard_map/all_gather | solution.py:21
  79.2 2.3 slice.66
  81.6 15.6 %slice.61 = f32[4480,1152]{1,0:T(8,128)} slice(f32[4608,1152]{1,0:T(8,128)} %param.4), slice={[128:4608], [0:1152]} | slice | bytes 41287680 | tf_op jit(solution)/shard_map/slice | solution.py:29
  97.2 22.6 %copy.88 = f32[4480,1152]{0,1:T(8,128)} copy(f32[4480,1152]{1,0:T(8,128)} %slice.61) | data formatting | bytes 41287680
  121.2 8.1 %while.6 = (s32[]{:T(128)}, f32[512,512]{0,1:T(8,128)S(1)}, s32[4,2]{0,1:T(2,128)S(1)}, f32[4,128,128]{2,1,0:T(8,128)S(1)}, s32[]{:T(128)}) while((s32[]{:T(128)}, f32[512,512]{0,1:T(8,128)S(1)}, s32[4,2]{0,1:T(2,128)S(1)}, f32[4,128,128]{2,1,0:T(8,128)S(1)}, s32[]{:T(128)}) %tuple.54), condition=%wide.while_cond, body=%wide.while_body.sunk | while | flops 2 | bytes 393321 | solution.py:27
  129.3 39.3 %custom-call.5 = f32[4,128,128]{1,2,0:T(8,128)S(1)} custom-call(f32[4,128,128]{2,1,0:T(8,128)S(1)} %get-tuple-element.26), custom_call_target="InvertDiagBlocksLowerTriangular" | custom-call | tf_op jit(solution)/shard_map/jit(_solve_triangular)/triangular_solve | solution.py:27
  174.5 2.2 convolution_subtract_fusion.2
  177.5 44.4 %all-gather.25.cloned.1.call-done = f32[35840,64]{0,1:T(8,128)} async-done(((f32[4480,64]{0,1:T(8,128)}), f32[35840,64]{0,1:T(8,128)}) %all-gather.25.cloned.1.call-update) | async-done | bytes 9175056 | tf_op jit(solution)/shard_map/all_gather | solution.py:40
  221.8 5.2 copy.89
  227.1 5.3 copy.57
  232.4 41.2 %fusion = f32[4480,1152]{0,1:T(8,128)S(1)} fusion(f32[4480,1152]{0,1:T(8,128)} %copy.88, f32[4480,512]{0,1:T(8,128)} %bitcast.114, f32[128,1152]{1,0:T(8,128)S(1)} %fusion.50, f32[128,1152]{1,0:T(8,128)S(1)} %fusion.51, f32[128,1152]{1,0:T(8,128)S(1)} %fusion.53, f32[128,1152]{1,0:T(8,128)S(1)} %fusion.34), kind=kOutput, calls=%fused_computation.9 | convolution fusion | flops 31715868672 | bytes 52822016 | tf_op jit(solution)/shard_map/dot_general | solution.py:32
  273.5 7.4 %copy-done = f32[4480,1152]{0,1:T(8,128)} copy-done((f32[4480,1152]{0,1:T(8,128)}, f32[4480,1152]{0,1:T(8,128)S(1)}, u32[]{:S(2)}) %copy-start) | copy-done | bytes 20643864
  281.9 34.4 %all_gather.53 = f32[128,512]{0,1:T(8,128)} all-gather(f32[128,64]{0,1:T(8,128)S(1)} %get-tuple-element.71), channel_id=1, replica_groups=mesh['row'=4,'col'=8] {'col'}, dimensions={1}, use_global_device_ids=true | all-gather | bytes 294912 | tf_op jit(solution)/shard_map/all_gather | solution.py:21
  316.4 2.3 slice.69
  318.8 2.3 fusion.28
  321.2 11.7 %while.7 = (s32[]{:T(128)}, f32[512,512]{0,1:T(8,128)}, s32[4,2]{0,1:T(2,128)S(1)}, f32[4,128,128]{2,1,0:T(8,128)S(1)}, s32[]{:T(128)}) while((s32[]{:T(128)}, f32[512,512]{0,1:T(8,128)}, s32[4,2]{0,1:T(2,128)S(1)}, f32[4,128,128]{2,1,0:T(8,128)S(1)}, s32[]{:T(128)}) %tuple.81), condition=%wide.while_cond.clone, body=%wide.while_body.clone.sunk | while | flops 2 | bytes 393321 | solution.py:27
  321.8 2.2 dynamic-slice.19
  324.8 2.2 dynamic-slice.19
  327.7 2.2 dynamic-slice.19
  330.6 2.1 dynamic-slice.19
  332.9 39.5 %custom-call.6 = f32[4,128,128]{1,2,0:T(8,128)S(1)} custom-call(f32[4,128,128]{2,1,0:T(8,128)S(1)} %get-tuple-element.27), custom_call_target="InvertDiagBlocksLowerTriangular" | custom-call | tf_op jit(solution)/shard_map/jit(_solve_triangular)/triangular_solve | solution.py:27
  374.3 6.2 copy.90
  380.4 6.2 copy.66
  386.6 11.8 %all-gather.19.cloned.1.call-done = f32[512,1152]{0,1:T(8,128)} async-done(((f32[128,1152]{0,1:T(8,128)}), f32[512,1152]{0,1:T(8,128)}) %all-gather.19.cloned.1.call-update) | async-done | bytes 2359312 | tf_op jit(solution)/shard_map/all_gather | solution.py:26
  401.3 2.2 convolution_subtract_fusion.6
  405.3 3.2 convolution_subtract_fusion.5
  411.1 4.8 convolution_subtract_fusion.1
  417.4 41.4 %fusion.2 = f32[4352,1152]{0,1:T(8,128)} fusion(f32[4352,512]{0,1:T(8,128)} %bitcast.117, f32[4480,1152]{0,1:T(8,128)} %copy-done, f32[128,1152]{0,1:T(8,128)S(1)} %fusion.46, f32[128,1152]{0,1:T(8,128)S(1)} %copy-done.7, f32[128,1152]{0,1:T(8,128)S(1)} %copy-done.5, f32[128,1152]{0,1:T(8,128)S(1)} %copy-done.3), kind=kOutput, calls=%fused_computation.11 | convolution fusion | flops 30809751552 | bytes 51380224 | tf_op jit(solution)/shard_map/dot_general | solution.py:32
  458.8 1.9 slice.87
  460.8 2.4 fusion.27
  463.2 12.1 %while.8 = (s32[]{:T(128)}, f32[512,512]{0,1:T(8,128)}, s32[4,2]{0,1:T(2,128)S(1)}, f32[4,128,128]{2,1,0:T(8,128)S(1)}, s32[]{:T(128)}) while((s32[]{:T(128)}, f32[512,512]{0,1:T(8,128)}, s32[4,2]{0,1:T(2,128)S(1)}, f32[4,128,128]{2,1,0:T(8,128)S(1)}, s32[]{:T(128)}) %tuple.82), condition=%wide.while_cond.clone.1, body=%wide.while_body.clone.1.sunk | while | flops 2 | bytes 393321 | solution.py:27
  463.8 2.3 dynamic-slice.21
  466.8 2.3 dynamic-slice.21
  469.9 2.3 dynamic-slice.21
  472.9 2.2 dynamic-slice.21
  475.3 39.5 %custom-call.7 = f32[4,128,128]{1,2,0:T(8,128)S(1)} custom-call(f32[4,128,128]{2,1,0:T(8,128)S(1)} %get-tuple-element.28), custom_call_target="InvertDiagBlocksLowerTriangular" | custom-call | tf_op jit(solution)/shard_map/jit(_solve_triangular)/triangular_solve | solution.py:27
  516.1 30.7 %all-gather.29.cloned.1.call-done = f32[33792,64]{0,1:T(8,128)} async-done(((f32[4224,64]{0,1:T(8,128)}), f32[33792,64]{0,1:T(8,128)}) %all-gather.29.cloned.1.call-update) | async-done | bytes 8650768 | tf_op jit(solution)/shard_map/all_gather | solution.py:40
  546.7 5.0 copy.91
  551.8 5.0 copy.74
  557.9 13.0 %all-gather.23.cloned.1.call-done = f32[512,1152]{0,1:T(8,128)} async-done(((f32[128,1152]{0,1:T(8,128)}), f32[512,1152]{0,1:T(8,128)}) %all-gather.23.cloned.1.call-update) | async-done | bytes 2359312 | tf_op jit(solution)/shard_map/all_gather | solution.py:26
  572.9 2.2 convolution_subtract_fusion.4
  576.1 3.2 convolution_subtract_fusion.3
  580.2 4.5 convolution_subtract_fusion
  586.5 41.0 %fusion.1 = f32[4224,1152]{0,1:T(8,128)} fusion(f32[4224,512]{0,1:T(8,128)} %bitcast.119, f32[4352,1152]{0,1:T(8,128)} %fusion.2, f32[128,1152]{0,1:T(8,128)S(1)} %fusion.42, f32[128,1152]{0,1:T(8,128)S(1)} %copy.72, f32[128,1152]{0,1:T(8,128)S(1)} %copy.71, f32[128,1152]{0,1:T(8,128)S(1)} %copy.70), kind=kOutput, calls=%fused_computation.10 | convolution fusion | flops 29903634432 | bytes 49938432 | tf_op jit(solution)/shard_map/dot_general | solution.py:32
  627.5 15.0 %pad_maximum_fusion = f32[4608,1152]{0,1:T(8,128)} fusion(f32[4224,1152]{0,1:T(8,128)} %fusion.1, f32[128,1152]{0,1:T(8,128)S(1)} %constant_dynamic-slice_fusion.3, f32[128,1152]{0,1:T(8,128)S(1)} %copy-done.12, f32[128,1152]{0,1:T(8,128)S(1)} %copy-done.11), kind=kLoop, calls=%fused_computation.12 | loop fusion | flops 15925248 | bytes 42467328 | tf_op jit(solution)/shard_map/concatenate | solution.py:44
  642.5 22.1 %copy.76 = f32[4608,1152]{1,0:T(8,128)} copy(f32[4608,1152]{0,1:T(8,128)} %pad_maximum_fusion) | data formatting | bytes 42467328 | tf_op jit(solution)/shard_map/concatenate | solution.py:44
  (142 shorter events, 44.5 us)
Async XLA Ops:
  6.5 113.2 %all-gather.13.cloned.1.call-start = ((), (), s32[]{:S(2)}) async-start(), calls=%async_computation | async-start | bytes 1310720 | tf_op jit(solution)/shard_map/all_gather | solution.py:24
  41.9 126.7 %all-gather.15.cloned.1.call-start = ((), (), s32[]{:S(2)}) async-start(), calls=%async_computation.1 | async-start | bytes 2949120 | tf_op jit(solution)/shard_map/all_gather | solution.py:26
  43.9 177.9 %all-gather.25.cloned.1.call-start = ((), (), s32[]{:S(2)}) async-start(), calls=%async_computation.6 | async-start | bytes 10321920 | tf_op jit(solution)/shard_map/all_gather | solution.py:40
  46.3 272.5 %all-gather.17.cloned.1.call-start = ((), (), s32[]{:S(2)}) async-start(), calls=%async_computation.2 | async-start | bytes 1310720 | tf_op jit(solution)/shard_map/all_gather | solution.py:24
  79.2 295.1 %all-gather.27.cloned.1.call-start = ((), (), s32[]{:S(2)}) async-start(), calls=%async_computation.7 | async-start | bytes 10027008 | tf_op jit(solution)/shard_map/all_gather | solution.py:40
  81.6 316.8 %all-gather.19.cloned.1.call-start = ((), (), s32[]{:S(2)}) async-start(), calls=%async_computation.3 | async-start | bytes 2949120 | tf_op jit(solution)/shard_map/all_gather | solution.py:26
  129.3 43.7 %copy-start.9 = (f32[512,512]{0,1:T(8,128)}, f32[512,512]{0,1:T(8,128)S(1)}, u32[]{:S(2)}) copy-start(f32[512,512]{0,1:T(8,128)S(1)} %get-tuple-element.226) | copy-start | bytes 3145732
  168.6 4.4 copy-start.10
  177.4 54.9 %copy-start.1 = (f32[128,1152]{1,0:T(8,128)}, f32[128,1152]{1,0:T(8,128)S(1)}, u32[]{:S(2)}) copy-start(f32[128,1152]{1,0:T(8,128)S(1)} %fusion.50) | copy-start | bytes 1769476
  273.5 7.4 %copy-start = (f32[4480,1152]{0,1:T(8,128)}, f32[4480,1152]{0,1:T(8,128)S(1)}, u32[]{:S(2)}) copy-start(f32[4480,1152]{0,1:T(8,128)S(1)} %fusion) | copy-start | bytes 61931524
  281.9 178.9 %all-gather.21.cloned.1.call-start = ((), (), s32[]{:S(2)}) async-start(), calls=%async_computation.4 | async-start | bytes 1310720 | tf_op jit(solution)/shard_map/all_gather | solution.py:24
  316.4 230.4 %all-gather.29.cloned.1.call-start = ((), (), s32[]{:S(2)}) async-start(), calls=%async_computation.8 | async-start | bytes 9732096 | tf_op jit(solution)/shard_map/all_gather | solution.py:40
  318.8 252.1 %all-gather.23.cloned.1.call-start = ((), (), s32[]{:S(2)}) async-start(), calls=%async_computation.5 | async-start | bytes 2949120 | tf_op jit(solution)/shard_map/all_gather | solution.py:26
  372.4 31.1 %copy-start.15 = (f32[4,128,128]{1,2,0:T(8,128)}, f32[4,128,128]{1,2,0:T(8,128)S(1)}, u32[]{:S(2)}) copy-start(f32[4,128,128]{1,2,0:T(8,128)S(1)} %custom-call.6) | copy-start | bytes 786436
  411.1 6.3 copy-start.3
  411.1 6.3 copy-start.5
  411.1 6.3 copy-start.7
  460.8 54.0 %copy-start.2 = (f32[128,1152]{1,0:T(8,128)S(1)}, f32[128,1152]{1,0:T(8,128)}, u32[]{:S(2)}) copy-start(f32[128,1152]{1,0:T(8,128)} %copy-done.1) | copy-start | bytes 1769476
  514.8 56.1 %copy-start.13 = (f32[4,128,128]{1,2,0:T(8,128)}, f32[4,128,128]{1,2,0:T(8,128)S(1)}, u32[]{:S(2)}) copy-start(f32[4,128,128]{1,2,0:T(8,128)S(1)} %custom-call.7) | copy-start | bytes 786436
  551.7 5.0 copy-start.4
  551.7 5.0 copy-start.6
  551.7 5.0 copy-start.8
  572.6 2.5 copy-start.14
  586.5 41.1 %copy-start.11 = (f32[128,1152]{0,1:T(8,128)S(1)}, f32[128,1152]{0,1:T(8,128)}, u32[]{:S(2)}) copy-start(f32[128,1152]{0,1:T(8,128)} %copy.75) | copy-start | bytes 1769476
  586.5 41.1 %copy-start.12 = (f32[128,1152]{0,1:T(8,128)S(1)}, f32[128,1152]{0,1:T(8,128)}, u32[]{:S(2)}) copy-start(f32[128,1152]{0,1:T(8,128)} %constant_dynamic-slice_fusion.4) | copy-start | bytes 1769476
Sparse Core Ops, SparseCore 0:
  42.0 17.7 all-gather.12
  61.3 24.0 all-gather.14
  87.6 134.2 all-gather.24
  223.2 15.0 all-gather.16
  240.3 133.8 all-gather.26
  375.7 22.6 all-gather.18
  400.0 16.8 all-gather.20
  419.0 127.6 all-gather.28
  548.3 22.5 all-gather.22
